TPU v7x, 256 devices: a whole 4x4x8 slice. The times are simulated.
256 devices in a mesh: seq: 32 (over y, x, core), head: 8 (over z).
Axes of the slice: x: 4, y: 4, z: 8, core: 2. Of those that a mesh axis runs over, the one named last changes fastest.
Arguments:
- tokens: bfloat16 [32768, 2048], P(('seq', 'head')), may hold values from -6 to 6
- w_qkv: bfloat16 [2048, 3, 2048], P(None, None, 'head'), may hold values from -0.125 to 0.125
- w_beta: bfloat16 [2048, 16], P(None, 'head'), may hold values from -0.125 to 0.125
- beta_bias: float32 [16], P('head'), may hold values from -8 to 2
- w_out: bfloat16 [2048, 2048], P('head'), may hold values from -0.125 to 0.125
Outputs:
- mixed: bfloat16 [32768, 2048], P(('seq', 'head'))
All inputs are finite; a program needn't handle non-finite values.
Results may differ from a plain program's by a relative error of at most 0.015.
Values may be sent and summed in bfloat16 or wider, within the bound.
A program may use at most 64 MiB of HBM per device.

v0:
```python
import jax
import jax.numpy as jnp
from jax import lax
from jax.sharding import PartitionSpec as P

C = 64
epsilon = 1e-06


def unit_norm(values):
    return values * lax.rsqrt(jnp.sum(values * values, -1, keepdims=True) + epsilon)


def prepare(queries, key_rows, value_rows, strength):
    highest = lax.Precision.HIGHEST
    size_k = key_rows.shape[-1]
    similar = jnp.einsum("...id,...jd->...ij", key_rows, key_rows, precision=highest)
    system = jnp.eye(C, dtype=jnp.float32) + jnp.tril(similar * strength[..., :, None], -1)
    weighted = jnp.concatenate(
        [strength[..., None] * key_rows, strength[..., None] * value_rows], -1
    )
    solved = jax.scipy.linalg.solve_triangular(system, weighted, lower=True, unit_diagonal=True)
    w_fac = solved[..., :size_k]
    u_fac = solved[..., size_k:]
    masked = jnp.tril(jnp.einsum("...id,...jd->...ij", queries, key_rows, precision=highest))
    q_eff = queries - jnp.einsum("...ij,...jd->...id", masked, w_fac, precision=highest)
    return (w_fac, u_fac, masked, q_eff)


def body(tokens, w_qkv, w_beta, beta_bias, w_out):
    highest = lax.Precision.HIGHEST
    float_tokens = tokens.astype(jnp.float32)
    normed = (
        float_tokens * lax.rsqrt(jnp.mean(float_tokens * float_tokens, -1, keepdims=True) + epsilon)
    ).astype(jnp.bfloat16)
    gathered = lax.all_gather(normed, "head", axis=0, tiled=True)
    length = gathered.shape[0]
    model_width = gathered.shape[1]
    local_heads = beta_bias.shape[0]
    size_k = w_out.shape[0] // local_heads
    projected = jnp.dot(
        gathered, w_qkv.reshape(model_width, -1), preferred_element_type=jnp.float32
    )
    projected = projected.reshape(length, 3, local_heads, size_k)
    queries = unit_norm(jax.nn.silu(projected[:, 0]))
    key_rows = unit_norm(jax.nn.silu(projected[:, 1]))
    value_rows = jax.nn.silu(projected[:, 2])
    strength = jax.nn.sigmoid(
        jnp.dot(gathered, w_beta, preferred_element_type=jnp.float32) + beta_bias
    )
    block_count = length // C

    def blocks(values):
        return values.reshape(block_count, C, local_heads, -1).transpose(0, 2, 1, 3)

    key_blocks = blocks(key_rows)
    w_fac, u_fac, masked, q_eff = prepare(
        blocks(queries),
        key_blocks,
        blocks(value_rows),
        strength.reshape(block_count, C, local_heads).transpose(0, 2, 1),
    )
    identity = jnp.broadcast_to(jnp.eye(size_k, dtype=jnp.float32), (local_heads, size_k, size_k))
    empty_state = jnp.zeros((local_heads, size_k, size_k), jnp.float32)

    def advance(pair_state, pieces):
        transition, state = pair_state
        w_blk, u_blk, m_blk, qe_blk, k_blk = pieces
        local_out = jnp.einsum("hcj,hvj->hcv", qe_blk, state, precision=highest) + jnp.einsum(
            "hcd,hdv->hcv", m_blk, u_blk, precision=highest
        )
        fold_query = jnp.einsum("hcj,hij->hci", qe_blk, transition, precision=highest)
        trans_w = jnp.einsum("hij,hcj->hic", transition, w_blk, precision=highest)
        new_transition = transition - jnp.einsum("hic,hcd->hid", trans_w, k_blk, precision=highest)
        state_w = jnp.einsum("hvj,hcj->hvc", state, w_blk, precision=highest)
        change = u_blk.transpose(0, 2, 1) - state_w
        new_state = state + jnp.einsum("hvc,hcd->hvd", change, k_blk, precision=highest)
        return ((new_transition, new_state), (local_out, fold_query))

    (trans_end, state_end), (local_all, fold_all) = lax.scan(
        advance, (identity, empty_state), (w_fac, u_fac, masked, q_eff, key_blocks)
    )
    all_trans, all_state = (
        lax.all_gather(trans_end[None].astype(jnp.bfloat16), "seq", axis=0, tiled=True).astype(
            jnp.float32
        ),
        lax.all_gather(state_end[None].astype(jnp.bfloat16), "seq", axis=0, tiled=True).astype(
            jnp.float32
        ),
    )
    own_index = lax.axis_index("seq")

    def chain_step(state, pieces):
        transition, partial_value, position = pieces
        advanced = jnp.einsum("hvj,hjk->hvk", state, transition, precision=highest) + partial_value
        return (jnp.where(position < own_index, advanced, state), None)

    incoming, _ = lax.scan(
        chain_step,
        empty_state,
        (all_trans, all_state, jnp.arange(all_trans.shape[0], dtype=jnp.int32)),
    )
    outputs = local_all + jnp.einsum("nhci,hvi->nhcv", fold_all, incoming, precision=highest)
    outputs = outputs.transpose(0, 2, 1, 3).reshape(length, local_heads, size_k)
    outputs = outputs * lax.rsqrt(jnp.mean(outputs * outputs, -1, keepdims=True) + epsilon)
    flat_out = outputs.reshape(length, local_heads * size_k).astype(jnp.bfloat16)
    return lax.psum_scatter(
        jnp.dot(flat_out, w_out, preferred_element_type=jnp.float32).astype(jnp.bfloat16),
        "head",
        scatter_dimension=0,
        tiled=True,
    )


def solution(mesh):
    return jax.shard_map(
        body,
        mesh=mesh,
        in_specs=(
            P(("seq", "head"), None),
            P(None, None, "head"),
            P(None, "head"),
            P("head"),
            P("head", None),
        ),
        out_specs=P(("seq", "head"), None),
        check_vma=False,
    )
```

profile of v0, /device:TPU:1, one launch (start us, length us, event | category | flops | bytes accessed | tf_op | source)
XLA Modules:
  0.0 669.9 jit_solution(6696784962300135828)
XLA Ops:
  7.9 2.0 fusion.63
  10.0 4.8 copy.39
  14.8 53.6 %all-gather.6.cloned.1.call-done = bf16[1024,2048]{1,0:T(8,128)(2,1)} async-done(((bf16[128,2048]{1,0:T(8,128)(2,1)}), bf16[1024,2048]{1,0:T(8,128)(2,1)}) %all-gather.6.cloned.1.call-update) | async-done | bytes 4194320 | tf_op jit(solution)/shard_map/all_gather | solution.py:36
  68.4 6.2 fusion.45
  75.3 1.7 fusion.85
  77.2 3.4 fusion.61
  80.7 2.7 broadcast_multiply_fusion
  83.4 2.7 fusion.57
  86.1 158.7 %custom-call.4 = f32[16,2,1,64,64]{3,4,2,1,0:T(8,128)} custom-call(f32[16,2,1,64,64]{4,3,2,1,0:T(8,128)} %fusion.57), custom_call_target="InvertDiagBlocksLowerTriangular" | custom-call | tf_op jit(solution)/shard_map/jit(_solve_triangular)/vmap(vmap())/triangular_solve | solution.py:22
  244.9 3.5 fusion.47
  249.7 2.0 convolution_select_fusion
  251.7 2.4 convolution_subtract_fusion.2
  254.2 127.7 %while.28 = (s32[]{:T(128)}, f32[2,128,128]{2,1,0:T(8,128)S(1)}, f32[2,128,128]{2,1,0:T(8,128)S(1)}, f32[16,2,64,128]{3,2,0,1:T(8,128)}, f32[16,2,64,128]{3,2,0,...) while((s32[]{:T(128)}, f32[2,128,128]{2,1,0:T(8,128)S(1)}, ...), condition=%wide.region_4.5_spmd.clone, body=%wide.region_3.4_spmd.clone.sunk | while | flops 163774464 | bytes 2167433 | solution.py:80
  258.8 1.8 fusion.138
  263.5 1.7 fusion.137
  266.8 1.8 fusion.138
  271.5 1.7 fusion.137
  274.8 1.8 fusion.138
  279.5 1.7 fusion.137
  282.8 1.8 fusion.138
  287.5 1.7 fusion.137
  290.8 1.8 fusion.138
  298.7 1.8 fusion.138
  303.4 1.7 fusion.137
  306.7 1.8 fusion.138
  311.3 1.7 fusion.137
  314.6 1.8 fusion.138
  322.6 1.8 fusion.138
  330.6 1.8 fusion.138
  335.3 1.7 fusion.137
  338.6 1.8 fusion.138
  343.2 1.7 fusion.137
  346.5 1.8 fusion.138
  354.5 1.8 fusion.138
  359.2 1.7 fusion.137
  362.5 1.8 fusion.138
  367.2 1.7 fusion.137
  370.5 1.8 fusion.138
  375.1 1.7 fusion.137
  378.4 1.8 fusion.138
  383.3 47.1 %all-gather.8.cloned.1.call-done = bf16[64,128,128]{2,1,0:T(8,128)(2,1)} async-done(((bf16[2,128,128]{2,1,0:T(8,128)(2,1)}), bf16[64,128,128]{2,1,0:T(8,128)(2,1)}) %all-gather.8.cloned.1.call-update) | async-done | bytes 2097168 | tf_op jit(solution)/shard_map/all_gather | solution.py:84
  430.4 4.1 convert.3
  434.5 46.5 %all-gather.10.cloned.1.call-done = bf16[64,128,128]{2,1,0:T(8,128)(2,1)} async-done(((bf16[2,128,128]{2,1,0:T(8,128)(2,1)}), bf16[64,128,128]{2,1,0:T(8,128)(2,1)}) %all-gather.10.cloned.1.call-update) | async-done | bytes 2097168 | tf_op jit(solution)/shard_map/all_gather | solution.py:87
  481.0 4.1 convert.4
  485.1 115.8 %while.29 = (s32[]{:T(128)}, f32[2,128,128]{1,2,0:T(8,128)S(1)}, s32[32]{0:T(128)S(1)}, s32[]{:T(128)}, f32[32,2,128,128]{3,2,1,0:T(8,128)}, /*index=5*/f32[32,2,128,128]{3,2,1,0:T(8,128)}, s32[]{:T(128)}, s32[]{:T(128)}) while((s32[]{:T(128)}, f32[2,128,128]{1,2,0:T(8,128)S(1)}, s32[32]{0:T(128)S(1)}, s32[]{:T(128)}, ...), condition=%wide.region_6.7_spmd.clone, body=%wide.region_5.6_spmd.clone.sunk | while | flops 50462724 | bytes 1443959 | solution.py:98
  600.9 2.4 multiply_reduce_fusion
  605.6 3.2 convolution_convert_fusion
  608.9 54.4 %reduce-scatter.2.cloned.1.call-done = bf16[128,2048]{1,0:T(8,128)(2,1)} async-done(((bf16[1024,2048]{1,0:T(8,128)(2,1)}), bf16[128,2048]{1,0:T(8,128)(2,1)}) %reduce-scatter.2.cloned.1.call-update) | async-done | bytes 524304 | tf_op jit(solution)/shard_map/reduce_scatter | solution.py:107
  (293 shorter events, 179.7 us)
Async XLA Ops:
  6.5 599.1 %copy-start = (bf16[256,2048]{1,0:T(8,128)(2,1)S(1)}, bf16[256,2048]{1,0:T(8,128)(2,1)}, u32[]{:S(2)}) copy-start(bf16[256,2048]{1,0:T(8,128)(2,1)} %param.13) | copy-start | bytes 3145732
  6.5 61.9 %all-gather.6.cloned.1.call-start = ((), (), s32[]{:S(2)}) async-start(), calls=%async_computation.1 | async-start | bytes 4718592 | tf_op jit(solution)/shard_map/all_gather | solution.py:36
  9.9 420.6 %all-gather.8.cloned.1.call-start = ((), (), s32[]{:S(2)}) async-start(), calls=%async_computation.3 | async-start | bytes 2162688 | tf_op jit(solution)/shard_map/all_gather | solution.py:84
  75.3 1.8 copy-start.4
  75.3 1.8 copy-start.5
  248.4 1.3 copy-start.2
  251.7 2.5 copy-start.3
  382.5 98.5 %all-gather.10.cloned.1.call-start = ((), (), s32[]{:S(2)}) async-start(), calls=%async_computation.4 | async-start | bytes 2162688 | tf_op jit(solution)/shard_map/all_gather | solution.py:87
  383.3 280.0 %reduce-scatter.2.cloned.1.call-start = ((), (), s32[]{:S(2)}) async-start(), calls=%async_computation.2 | async-start | bytes 4718592 | tf_op jit(solution)/shard_map/reduce_scatter | solution.py:107
  485.1 115.8 %copy-start.1 = (f32[16,2,64,128]{3,2,0,1:T(8,128)S(1)}, f32[16,2,64,128]{3,2,0,1:T(8,128)}, u32[]{:S(2)}) copy-start(f32[16,2,64,128]{3,2,0,1:T(8,128)} %get-tuple-element.92) | copy-start | bytes 3145732
Sparse Core Ops, SparseCore 0:
  10.0 58.3 all-gather.5
  382.7 47.7 all-gather.7
  433.0 47.9 all-gather.9
  609.0 54.2 reduce-scatter.1
where the time goes:
time: 675 us; the launch traced here: 670 us
  waiting for transfers between devices  202 us (30%)
  matrix products  194 us (29%)
  other arithmetic  175 us (26%)
  local copies, waits for them, and re-layouts  61.9 us (9%)
  loops' own time  23.5 us (3%)
  between operations  13.4 us (2%)
    another operation x4, other arithmetic, prepare(): jax.scipy.linalg.solve_triangular(system, weighted, lower=True, unit_diag...  159 us
    reduce_scatter x1, waiting for transfers between devices, body(): lax.psum_scatter(jnp.dot(flat_out, w_out, preferred_element_type=jnp.floa...  54.4 us
    all_gather x1, waiting for transfers between devices, body(): gathered = lax.all_gather(normed, 'head', axis=0, tiled=True)  53.6 us
    dynamic_slice x96, local copies, waits for them, and re-layouts, body(): lax.scan(chain_step, empty_state, (all_trans, all_state, jnp.arange(all_t...  51.2 us
    all_gather x1, waiting for transfers between devices, body(): lax.all_gather(trans_end[None].astype(jnp.bfloat16), 'seq', axis=0, tiled...  47.1 us
    all_gather x1, waiting for transfers between devices, body(): lax.all_gather(state_end[None].astype(jnp.bfloat16), 'seq', axis=0, tiled...  46.5 us
    dot_general x32, matrix products, chain_step(): jnp.einsum('hvj,hjk->hvk', state, transition, precision=highest)  41.8 us
    dot_general x16, matrix products, advance(): jnp.einsum('hcj,hij->hci', qe_blk, transition, precision=highest)  29.4 us
  transfers between devices with their start and end apart: 4, of which 4 were waited for; matrix products, arithmetic and copies ran while one was open for 1% of the time, Pallas kernels for 0%

commit v1 on v0

--- a/solution.py
+++ b/solution.py
@@ -2,6 +2,7 @@
 import jax.numpy as jnp
 from jax import lax
 from jax.sharding import PartitionSpec as P
+from jax.lax import all_to_all, axis_size
 
 C = 64
 epsilon = 1e-06
@@ -80,13 +81,20 @@
     (trans_end, state_end), (local_all, fold_all) = lax.scan(
         advance, (identity, empty_state), (w_fac, u_fac, masked, q_eff, key_blocks)
     )
+    _begin_loads = lambda buf, which_axis: jnp.concatenate(
+        all_to_all(
+            jnp.stack([buf for _ in range(axis_size(which_axis))]),
+            axis_name=which_axis,
+            split_axis=0,
+            concat_axis=0,
+        ),
+        axis=0,
+    )
     all_trans, all_state = (
         lax.all_gather(trans_end[None].astype(jnp.bfloat16), "seq", axis=0, tiled=True).astype(
             jnp.float32
         ),
-        lax.all_gather(state_end[None].astype(jnp.bfloat16), "seq", axis=0, tiled=True).astype(
-            jnp.float32
-        ),
+        _begin_loads(state_end[None].astype(jnp.bfloat16), "seq").astype(jnp.float32),
     )
     own_index = lax.axis_index("seq")
 

time: 675 us -> 606 us (0.90)
  waiting for transfers between devices: 202 us -> 157 us
  local copies, waits for them, and re-layouts: 61.9 us -> 31.4 us
  starting transfers between devices: 0.13 us -> 7.78 us
    all_gather x1 -> x0, waiting for transfers between devices: 46.5 us -> none  [body(): lax.all_gather(state_end[None].astype(jnp.bfloat16), 'seq', axis=0, tiled...]
    dynamic_slice x96 -> x32, local copies, waits for them, and re-layouts: 51.2 us -> 18.8 us  [body(): lax.scan(chain_step, empty_state, (all_trans, all_state, jnp.arange(all_t...]
    all_to_all x0 -> x1, waiting for transfers between devices: none -> 29.7 us  [body(): all_to_all(jnp.stack([buf for _ in range(axis_size(which_axis))]), axis_n...]
    all_gather x1, waiting for transfers between devices: 47.1 us -> 18.8 us  [body(): lax.all_gather(trans_end[None].astype(jnp.bfloat16), 'seq', axis=0, tiled...]
    all_to_all x0 -> x1, starting transfers between devices: none -> 7.7 us  [body(): all_to_all(jnp.stack([buf for _ in range(axis_size(which_axis))]), axis_n...]
  transfers between devices with their start and end apart: 4 -> 4, of which waited for: 4 -> 4; matrix products, arithmetic and copies ran while one was open for 1% -> 2% of each run, Pallas kernels for 0% -> 0%
where the time goes in v1:
time: 606 us; the launch traced here: 601 us
  matrix products  196 us (32%)
  other arithmetic  173 us (29%)
  waiting for transfers between devices  157 us (26%)
  local copies, waits for them, and re-layouts  31.4 us (5%)
  loops' own time  23.1 us (4%)
  between operations  13.4 us (2%)
  starting transfers between devices  7.78 us (1%)
    another operation x4, other arithmetic, prepare(): jax.scipy.linalg.solve_triangular(system, weighted, lower=True, unit_diag...  159 us
    reduce_scatter x1, waiting for transfers between devices, body(): lax.psum_scatter(jnp.dot(flat_out, w_out, preferred_element_type=jnp.floa...  54.4 us
    all_gather x1, waiting for transfers between devices, body(): gathered = lax.all_gather(normed, 'head', axis=0, tiled=True)  53.6 us
    dot_general x32, matrix products, chain_step(): jnp.einsum('hvj,hjk->hvk', state, transition, precision=highest)  43.9 us
    all_to_all x1, waiting for transfers between devices, body(): all_to_all(jnp.stack([buf for _ in range(axis_size(which_axis))]), axis_n...  29.7 us
    dot_general x16, matrix products, advance(): jnp.einsum('hcj,hij->hci', qe_blk, transition, precision=highest)  29.2 us
    dot_general x16, matrix products, advance(): jnp.einsum('hcd,hdv->hcv', m_blk, u_blk, precision=highest)  26.6 us
    another operation x1, loops' own time, body(): lax.scan(chain_step, empty_state, (all_trans, all_state, jnp.arange(all_t...  22.1 us
  transfers between devices with their start and end apart: 4, of which 4 were waited for; matrix products, arithmetic and copies ran while one was open for 2% of the time, Pallas kernels for 0%

profile of v1, /device:TPU:1, one launch (start us, length us, event | category | flops | bytes accessed | tf_op | source)
XLA Modules:
  0.0 601.1 jit_solution(12823991996359406437)
XLA Ops:
  7.9 2.0 fusion.63
  10.0 4.7 copy.39
  14.8 53.6 %all-gather.4.cloned.1.call-done = bf16[1024,2048]{1,0:T(8,128)(2,1)} async-done(((bf16[128,2048]{1,0:T(8,128)(2,1)}), bf16[1024,2048]{1,0:T(8,128)(2,1)}) %all-gather.4.cloned.1.call-update) | async-done | bytes 4194320 | tf_op jit(solution)/shard_map/all_gather | solution.py:37
  68.4 6.2 %fusion.45 = f32[1024,3,2,128]{3,0,2,1:T(8,128)S(1)} fusion(bf16[3,2,128,2048]{3,2,1,0:T(8,128)(2,1)} %bitcast.200, bf16[1024,2048]{1,0:T(8,128)(2,1)} %all-gather.4.cloned.1.call-done), kind=kOutput, calls=%fused_computation.51 | convolution fusion | flops 3221225472 | bytes 10485760 | tf_op jit(solution)/shard_map/dot_general | solution.py:42
  75.3 1.7 fusion.85
  77.2 3.4 fusion.61
  80.7 2.7 broadcast_multiply_fusion
  83.4 2.8 fusion.57
  86.1 158.7 %custom-call.4 = f32[16,2,1,64,64]{3,4,2,1,0:T(8,128)} custom-call(f32[16,2,1,64,64]{4,3,2,1,0:T(8,128)} %fusion.57), custom_call_target="InvertDiagBlocksLowerTriangular" | custom-call | tf_op jit(solution)/shard_map/jit(_solve_triangular)/vmap(vmap())/triangular_solve | solution.py:23
  244.9 3.5 fusion.47
  249.7 2.0 convolution_select_fusion
  251.7 2.4 convolution_subtract_fusion.2
  254.2 127.3 %while.28 = (s32[]{:T(128)}, f32[2,128,128]{2,1,0:T(8,128)S(1)}, f32[2,128,128]{2,1,0:T(8,128)S(1)}, f32[16,2,64,128]{3,2,0,1:T(8,128)}, f32[16,2,64,128]{3,2,0,...) while((s32[]{:T(128)}, f32[2,128,128]{2,1,0:T(8,128)S(1)}, ...), condition=%wide.region_4.5_spmd.clone, body=%wide.region_3.4_spmd.clone.sunk | while | flops 163774464 | bytes 2167433 | solution.py:81
  255.6 1.7 fusion.137
  258.9 1.8 fusion.138
  266.8 1.8 fusion.138
  274.7 1.8 fusion.138
  279.4 1.7 fusion.137
  282.7 1.8 fusion.138
  290.6 1.8 fusion.138
  295.3 1.7 fusion.137
  298.6 1.8 fusion.138
  306.5 1.8 fusion.138
  314.5 1.8 fusion.138
  322.4 1.8 fusion.138
  327.1 1.7 fusion.137
  330.4 1.8 fusion.138
  338.3 1.8 fusion.138
  343.0 1.7 fusion.137
  346.3 1.8 fusion.138
  350.9 1.7 fusion.137
  354.2 1.8 fusion.138
  358.9 1.7 fusion.137
  362.2 1.8 fusion.138
  366.8 1.7 fusion.137
  370.1 1.8 fusion.138
  374.8 1.7 fusion.137
  378.0 1.8 fusion.138
  382.3 1.8 stack.2
  384.1 7.7 %all-to-all-start = ((bf16[32,1,2,128,128]{3,4,2,1,0:T(8,128)(2,1)}), bf16[32,1,2,128,128]{3,4,2,1,0:T(8,128)(2,1)S(1)}, u32[]{:S(2)}, u32[]{:S(2)}) async-start(bf16[32,1,2,128,128]{3,4,2,1,0:T(8,128)(2,1)} %stack.2), calls=%async_computation | async-start | bytes 4194304 | tf_op jit(solution)/shard_map/all_to_all | solution.py:85
  391.9 29.7 %all-to-all-done = bf16[32,1,2,128,128]{3,4,2,1,0:T(8,128)(2,1)S(1)} async-done(((bf16[32,1,2,128,128]{3,4,2,1,0:T(8,128)(2,1)}), bf16[32,1,2,128,128]{3,4,2,1,0:T(8,128)(2,1)S(1)}, u32[]{:S(2)}, u32[]{:S(2)}) %all-to-all-start) | async-done | bytes 2097184 | tf_op jit(solution)/shard_map/all_to_all | solution.py:85
  421.6 2.5 bitcast_convert_fusion
  424.1 18.8 %all-gather.6.cloned.1.call-done = bf16[64,128,128]{2,1,0:T(8,128)(2,1)} async-done(((bf16[2,128,128]{2,1,0:T(8,128)(2,1)}), bf16[64,128,128]{2,1,0:T(8,128)(2,1)}) %all-gather.6.cloned.1.call-update) | async-done | bytes 2097168 | tf_op jit(solution)/shard_map/all_gather | solution.py:94
  442.9 4.2 convert.4
  447.1 85.0 %while.29 = (s32[]{:T(128)}, f32[2,128,128]{1,2,0:T(8,128)S(1)}, s32[32]{0:T(128)S(1)}, s32[]{:T(128)}, f32[32,2,128,128]{3,2,1,0:T(8,128)}, /*index=5*/f32[32,2,128,128]{2,3,1,0:T(8,128)}, s32[]{:T(128)}, s32[]{:T(128)}) while((s32[]{:T(128)}, f32[2,128,128]{1,2,0:T(8,128)S(1)}, s32[32]{0:T(128)S(1)}, s32[]{:T(128)}, ...), condition=%wide.region_6.7_spmd.clone, body=%wide.region_5.6_spmd.clone.sunk | while | flops 50462724 | bytes 920179 | solution.py:106
  532.1 2.4 multiply_reduce_fusion
  536.9 3.2 convolution_convert_fusion
  540.2 54.4 %reduce-scatter.2.cloned.1.call-done = bf16[128,2048]{1,0:T(8,128)(2,1)} async-done(((bf16[1024,2048]{1,0:T(8,128)(2,1)}), bf16[128,2048]{1,0:T(8,128)(2,1)}) %reduce-scatter.2.cloned.1.call-update) | async-done | bytes 524304 | tf_op jit(solution)/shard_map/reduce_scatter | solution.py:115
  (230 shorter events, 151.9 us)
Async XLA Ops:
  6.5 530.4 %copy-start = (bf16[256,2048]{1,0:T(8,128)(2,1)S(1)}, bf16[256,2048]{1,0:T(8,128)(2,1)}, u32[]{:S(2)}) copy-start(bf16[256,2048]{1,0:T(8,128)(2,1)} %param.13) | copy-start | bytes 3145732
  6.5 61.9 %all-gather.4.cloned.1.call-start = ((), (), s32[]{:S(2)}) async-start(), calls=%async_computation.2 | async-start | bytes 4718592 | tf_op jit(solution)/shard_map/all_gather | solution.py:37
  9.9 433.0 %all-gather.6.cloned.1.call-start = ((), (), s32[]{:S(2)}) async-start(), calls=%async_computation.4 | async-start | bytes 2162688 | tf_op jit(solution)/shard_map/all_gather | solution.py:94
  75.3 1.9 copy-start.4
  75.3 1.9 copy-start.5
  248.4 1.3 copy-start.2
  251.7 2.5 copy-start.3
  384.1 37.4 %all-to-all-start = ((bf16[32,1,2,128,128]{3,4,2,1,0:T(8,128)(2,1)}), bf16[32,1,2,128,128]{3,4,2,1,0:T(8,128)(2,1)S(1)}, u32[]{:S(2)}, u32[]{:S(2)}) async-start(bf16[32,1,2,128,128]{3,4,2,1,0:T(8,128)(2,1)} %stack.2), calls=%async_computation | async-start | bytes 4194304 | tf_op jit(solution)/shard_map/all_to_all | solution.py:85
  391.8 202.7 %reduce-scatter.2.cloned.1.call-start = ((), (), s32[]{:S(2)}) async-start(), calls=%async_computation.3 | async-start | bytes 4718592 | tf_op jit(solution)/shard_map/reduce_scatter | solution.py:115
  442.9 89.2 %copy-start.1 = (f32[16,2,64,128]{3,2,0,1:T(8,128)S(1)}, f32[16,2,64,128]{3,2,0,1:T(8,128)}, u32[]{:S(2)}) copy-start(f32[16,2,64,128]{3,2,0,1:T(8,128)} %get-tuple-element.92) | copy-start | bytes 3145732
Sparse Core Ops, SparseCore 0:
  10.0 58.3 all-gather.3
  382.3 60.6 all-gather.5
  540.3 54.2 reduce-scatter.1
